TPU v7x, 32 devices: a whole 2x2x4 slice. The times are simulated.
32 devices in a mesh: group: 2 (over y), expert: 4 (over z), dp: 4 (over x, core).
Axes of the slice: x: 2, y: 2, z: 4, core: 2. Of those that a mesh axis runs over, the one named last changes fastest.
Arguments:
- tokens: bfloat16 [256, 4096], P(('group', 'expert', 'dp')), parts along dimension 0, may hold values from -6 to 6
- routing: int32 [256, 8], P(('group', 'expert', 'dp')), parts along dimension 0, may hold values from 0 to 127, as said below
- gate_quantized: int32 [256, 8], P(('group', 'expert', 'dp')), parts along dimension 0, may hold values from 1 to 32767
- tenant: int32 [256], P(('group', 'expert', 'dp')), parts along dimension 0, may hold values from 0 to 23
- tenant_page_lookup: int32 [4, 24], replicated, may hold values from 0 to 23, each once within a row
- gate_weight: bfloat16 [4, 4096, 1024], P('expert', None, 'dp'), may hold values from -0.09375 to 0.09375
- up_projection: bfloat16 [4, 4096, 1024], P('expert', None, 'dp'), may hold values from -0.09375 to 0.09375
- down_weight: bfloat16 [4, 1024, 4096], P('expert', None, 'dp'), may hold values from -0.1875 to 0.1875
- adapter_shrink: bfloat16 [4, 24, 16, 4096], P('expert', 'dp'), may hold values from -0.09375 to 0.09375
- adapter_expand: bfloat16 [4, 24, 16, 1024], P('expert', 'dp'), may hold values from -1.5 to 1.5
Outputs:
- mixed_out: bfloat16 [256, 4096], P(('group', 'expert', 'dp')), parts along dimension 0
There are 2 independent parts, one for each index of `group`. A program takes and returns all parts, laid end to end along the dimension named above; an argument that names none is the same for every part. Nothing has to cross between parts.
Inputs may be any that keep to these rules, and one draw needn't show every extreme that they name: `routing`: each row names 8 different experts. Among the 8 tokens of one device no expert is named more than 2 times, and in every draw some expert below 4 is named exactly 2 times by the tokens of every device. `tenant_page_lookup`: row e gives every tenant a different page of expert e's pool.
All inputs are finite; a program needn't handle non-finite values.
Results may differ from a plain program's by a relative error of at most 0.0061.
Values may be sent and summed in bfloat16 or wider, within the bound.
A program may use at most 64 MiB of HBM per device.

v0:
```python
import jax
import jax.numpy as jnp
from jax import lax
from jax.sharding import PartitionSpec as P


def slot_tables(routing, experts, capacity):
    expert_ids = jnp.arange(experts, dtype=jnp.int32)
    matches = routing[:, :, None] == expert_ids[None, None, :]
    assign = jnp.sum(matches.astype(jnp.int32), axis=1)
    slot_rank = jnp.cumsum(assign, axis=0) - assign
    scale_levels = jnp.arange(capacity, dtype=jnp.int32)
    placing = (assign.T[:, None, :] == 1) & (slot_rank.T[:, None, :] == scale_levels[None, :, None])
    return (matches, slot_rank, placing)


def per_device(
    tokens,
    routing,
    gate_quantized,
    tenant,
    tenant_page_lookup,
    gate_weight,
    up_projection,
    down_weight,
    adapter_shrink,
    adapter_expand,
):
    tok_count, model_width = tokens.shape
    experts, tenants = tenant_page_lookup.shape
    capacity = tok_count // 4
    rank_extent = adapter_shrink.shape[2]
    part_width = down_weight.shape[2]
    my_expert = lax.axis_index("expert")
    matches, slot_rank, placing = slot_tables(routing, experts, capacity)
    send_rows = jnp.einsum(
        "ect,td->ecd", placing.astype(jnp.bfloat16), tokens, preferred_element_type=jnp.float32
    ).astype(jnp.bfloat16)
    send_ten = jnp.sum(placing.astype(jnp.int32) * (tenant[None, None, :] + 1), axis=2)
    got_rows, got_ten = (
        lax.all_to_all(send_rows, "expert", split_axis=0, concat_axis=0, tiled=True),
        lax.all_to_all(send_ten, "expert", split_axis=0, concat_axis=0, tiled=True),
    )
    slot_rows, slot_ten = (
        lax.all_gather(got_rows[None], "dp", axis=0, tiled=True),
        lax.all_gather(got_ten[None], "dp", axis=0, tiled=True),
    )
    block_shape = slot_rows.shape[:3]
    slot_count = block_shape[0] * block_shape[1] * block_shape[2]
    slot_input = slot_rows.reshape(slot_count, model_width)
    slot_tenant = slot_ten.reshape(slot_count)
    page_row = lax.dynamic_index_in_dim(tenant_page_lookup, my_expert, 0, keepdims=False)
    tenant_ids = jnp.arange(tenants, dtype=jnp.int32)
    tenant_hot = slot_tenant[:, None] == tenant_ids[None, :] + 1
    slot_page = jnp.sum(jnp.where(tenant_hot, page_row[None, :], 0), axis=1)
    occupied = slot_tenant > 0
    page_pick = ((slot_page[:, None] == tenant_ids[None, :]) & occupied[:, None]).astype(
        jnp.float32
    )
    partial_terms = lax.all_gather(adapter_shrink, "dp", axis=1, tiled=True)
    page_count = partial_terms.shape[1]
    flat_pages = partial_terms.reshape(page_count * rank_extent, model_width)
    products = lax.dot_general(
        slot_input, flat_pages, (((1,), (1,)), ((), ())), preferred_element_type=jnp.float32
    )
    shrink_result = jnp.sum(
        page_pick[:, :, None] * products.reshape(slot_count, page_count, rank_extent), axis=1
    )
    shrink_low = shrink_result.astype(jnp.bfloat16)
    expand_every_page = lax.all_to_all(
        adapter_expand, "dp", split_axis=3, concat_axis=1, tiled=True
    )[0]
    hidden_part = expand_every_page.shape[2]
    expand_matrix = expand_every_page.reshape(tenants * rank_extent, hidden_part)
    spread_rows = (page_pick[:, :, None] * shrink_low.astype(jnp.float32)[:, None, :]).astype(
        jnp.bfloat16
    )
    spread_rows = spread_rows.reshape(slot_count, tenants * rank_extent)
    adapter_update = jnp.dot(spread_rows, expand_matrix, preferred_element_type=jnp.float32)
    gate_act = jnp.dot(slot_input, gate_weight[0], preferred_element_type=jnp.float32)
    up_activation = (
        jnp.dot(slot_input, up_projection[0], preferred_element_type=jnp.float32) + adapter_update
    )
    hidden = (jax.nn.silu(gate_act) * up_activation).astype(jnp.bfloat16)
    weights = down_weight[0]
    expert_out = jnp.dot(
        lax.all_gather(hidden, "dp", axis=1, tiled=True),
        weights,
        preferred_element_type=jnp.float32,
    )
    expert_out = expert_out.astype(jnp.bfloat16).reshape(block_shape + (part_width,))
    home_rows = lax.all_to_all(expert_out, "dp", split_axis=0, concat_axis=3, tiled=True)
    back_rows = lax.all_to_all(home_rows, "expert", split_axis=1, concat_axis=0, tiled=True)
    back_rows = back_rows.reshape(experts * capacity, model_width)
    chosen_rank = jnp.sum(jnp.where(matches, slot_rank[:, None, :], 0), axis=2)
    inside = routing < experts
    flat_index = routing * capacity + chosen_rank
    slot_ids = jnp.arange(experts * capacity, dtype=jnp.int32)
    row_picks = ((flat_index[:, :, None] == slot_ids[None, None, :]) & inside[:, :, None]).astype(
        jnp.bfloat16
    )
    picked = jnp.einsum("tkm,md->tkd", row_picks, back_rows, preferred_element_type=jnp.float32)
    mix_coef = jnp.where(inside, gate_quantized.astype(jnp.float32) / 32768.0, jnp.float32(0.0))
    mixed_out = jnp.sum(mix_coef[:, :, None] * picked, axis=1)
    return mixed_out.astype(jnp.bfloat16)


def solution(mesh):
    return jax.shard_map(
        per_device,
        mesh=mesh,
        in_specs=(
            P(("group", "expert", "dp"), None),
            P(("group", "expert", "dp"), None),
            P(("group", "expert", "dp"), None),
            P(("group", "expert", "dp")),
            P(),
            P("expert", None, "dp"),
            P("expert", None, "dp"),
            P("expert", None, "dp"),
            P("expert", "dp", None, None),
            P("expert", "dp", None, None),
        ),
        out_specs=P(("group", "expert", "dp"), None),
        check_vma=False,
    )
```

profile of v0, /device:TPU:0, one launch (start us, length us, event | category | flops | bytes accessed | tf_op | source)
XLA Modules:
  0.0 94.2 jit_solution(14872100671156031645)
XLA Ops:
  6.5 0.7 all-gather.4.cloned.1.call-update
  7.3 0.8 convert_reduce_fusion
  8.1 0.2 reduce_window_sum.11
  8.3 0.7 broadcast_add_fusion
  9.1 0.7 copy.39
  9.8 6.3 %all-to-all-start.1 = ((s32[4,1,2]{2,1,0:T(1,128)}), s32[4,1,2]{2,1,0:T(1,128)S(1)}, u32[]{:S(2)}, u32[]{:S(2)}) async-start(s32[4,1,2]{2,1,0:T(1,128)} %copy.39), calls=%async_computation.1 | async-start | bytes 4096 | tf_op jit(solution)/shard_map/all_to_all | solution.py:42
  16.1 1.0 %convolution_convert_fusion = bf16[4,2,4096]{2,0,1:T(4,128)(2,1)S(1)} fusion(bf16[8,4096]{1,0:T(8,128)(2,1)} %param.10, s32[4,8]{1,0:T(4,128)S(1)} %bitcast.58, pred[4,8]{1,0:T(4,128)(4,1)S(1)} %compare_bitcast_fusion), kind=kOutput, calls=%fused_computation.1 | convolution fusion | flops 557184 | bytes 131232 | tf_op jit(solution)/shard_map/ect,td->ecd/dot_general | solution.py:36
  17.1 0.7 copy.38
  17.8 3.3 %copy.43 = bf16[1,6,16,1024]{2,1,0,3:T(8,128)(2,1)} copy(bf16[1,6,16,1024]{3,2,1,0:T(8,128)(2,1)} %param.19) | data formatting | bytes 393216 | tf_op args[9]
  21.2 3.5 %reshape.122 = bf16[4,2,12288]{2,1,0:T(2,128)(2,1)} reshape(bf16[1024,1,6,16]{3,2,1,0:T(8,128)(2,1)} %bitcast.51) | data formatting | bytes 393216
  24.7 0.7 dynamic-slice_bitcast_fusion
  25.4 5.1 %all-to-all-start = ((bf16[4,2,4096]{2,1,0:T(2,128)(2,1)}), bf16[4,2,4096]{2,1,0:T(2,128)(2,1)S(1)}, u32[]{:S(2)}, u32[]{:S(2)}) async-start(bf16[4,2,4096]{2,1,0:T(2,128)(2,1)} %copy.38), calls=%async_computation | async-start | bytes 131072 | tf_op jit(solution)/shard_map/all_to_all | solution.py:41
  30.5 5.3 %all-gather.1 = s32[16,1,2]{2,1,0:T(1,128)S(1)} all-gather(s32[4,1,2]{2,1,0:T(1,128)S(1)} %all-to-all-done.1), channel_id=3, replica_groups=mesh['group'=2,'expert'=4,'dp'=4] {'dp'}, dimensions={0}, use_global_device_ids=true | all-gather | bytes 160 | tf_op jit(solution)/shard_map/all_gather | solution.py:46
  35.8 0.5 broadcast.74
  36.3 0.6 reduce.3
  37.1 3.4 %all-to-all-start.2 = ((bf16[4,2,12288]{2,1,0:T(2,128)(2,1)}), bf16[4,2,12288]{2,1,0:T(2,128)(2,1)S(1)}, u32[]{:S(2)}, u32[]{:S(2)}) async-start(bf16[4,2,12288]{2,1,0:T(2,128)(2,1)} %reshape.122), calls=%async_computation.2 | async-start | bytes 393216 | tf_op jit(solution)/shard_map/all_to_all | solution.py:70
  40.5 7.5 %all-gather = bf16[16,2,4096]{2,1,0:T(2,128)(2,1)S(1)} all-gather(bf16[4,2,4096]{2,1,0:T(2,128)(2,1)S(1)} %all-to-all-done), channel_id=2, replica_groups=mesh['group'=2,'expert'=4,'dp'=4] {'dp'}, dimensions={0}, use_global_device_ids=true | all-gather | bytes 327680 | tf_op jit(solution)/shard_map/all_gather | solution.py:45
  48.2 2.2 %fusion.5 = f32[32,256]{1,0:T(8,128)S(1)} fusion(bf16[32,4096]{1,0:T(8,128)(2,1)S(1)} %reshape.101, bf16[1,4096,256]{2,1,0:T(8,128)(2,1)} %param.16), kind=kOutput, calls=%fused_computation.7 | convolution fusion | flops 67108864 | bytes 2392064 | tf_op jit(solution)/shard_map/dot_general | solution.py:82
  50.5 0.5 fusion.7
  50.9 2.9 %reshape.123 = bf16[1024,1,6,16]{3,2,1,0:T(8,128)(2,1)} reshape(bf16[4,2,12288]{2,1,0:T(2,128)(2,1)S(1)} %all-to-all-done.2) | data formatting | bytes 393216
  53.9 2.5 %copy.48 = bf16[1,6,16,4,256]{4,3,2,1,0:T(4,128)(2,1)S(1)} copy(bf16[1,6,16,4,256]{2,1,4,3,0:T(8,128)(2,1)} %bitcast.50) | data formatting | bytes 393216 | tf_op jit(solution)/shard_map/all_to_all | solution.py:70
  56.4 4.2 %fusion.16 = bf16[32,16]{0,1:T(8,128)(2,1)S(1)} fusion(bf16[32,4096,1]{1,0,2:T(8,128)(2,1)S(1)} %reshape.109, bf16[1,24,16,4096]{3,2,0,1:T(8,128)(2,1)} %all-gather.4.cloned.1.call-done, f32[32,24]{0,1:T(8,128)S(1)} %fusion.27), kind=kOutput, calls=%fused_computation.14 | convolution fusion | flops 100687360 | bytes 3411968 | tf_op jit(solution)/shard_map/dot_general | solution.py:63
  60.7 0.2 fusion.20
  60.9 5.2 %all_gather.15 = bf16[32,1024]{1,0:T(8,128)(2,1)S(1)} all-gather(bf16[32,256]{1,0:T(8,128)(2,1)S(1)} %fusion.20), channel_id=1, replica_groups=mesh['group'=2,'expert'=4,'dp'=4] {'dp'}, dimensions={1}, use_global_device_ids=true | all-gather | bytes 81920 | tf_op jit(solution)/shard_map/all_gather | solution.py:87
  66.2 0.5 fusion.13
  66.6 0.7 reshape.102
  67.3 3.3 %all-to-all-start.3 = ((bf16[4,4,2,1024]{3,2,1,0:T(2,128)(2,1)}), bf16[4,4,2,1024]{3,2,1,0:T(2,128)(2,1)S(1)}, u32[]{:S(2)}, u32[]{:S(2)}) async-start(bf16[4,4,2,1024]{3,2,1,0:T(2,128)(2,1)} %reshape.102), calls=%async_computation.3 | async-start | bytes 131072 | tf_op jit(solution)/shard_map/all_to_all | solution.py:92
  70.7 4.0 %all-to-all-done.3 = bf16[4,4,2,1024]{3,2,1,0:T(2,128)(2,1)S(1)} async-done(((bf16[4,4,2,1024]{3,2,1,0:T(2,128)(2,1)}), bf16[4,4,2,1024]{3,2,1,0:T(2,128)(2,1)S(1)}, u32[]{:S(2)}, u32[]{:S(2)}) %all-to-all-start.3) | async-done | bytes 65568 | tf_op jit(solution)/shard_map/all_to_all | solution.py:92
  74.7 0.7 copy.49
  75.4 5.1 %all-to-all-start.4 = ((bf16[1,4,2,4096]{3,2,0,1:T(2,128)(2,1)}), bf16[1,4,2,4096]{3,2,0,1:T(2,128)(2,1)S(1)}, u32[]{:S(2)}, u32[]{:S(2)}) async-start(bf16[1,4,2,4096]{3,2,0,1:T(2,128)(2,1)} %bitcast.16), calls=%async_computation.4 | async-start | bytes 131072 | tf_op jit(solution)/shard_map/all_to_all | solution.py:93
  80.5 5.7 %all-to-all-done.4 = bf16[1,4,2,4096]{3,2,0,1:T(2,128)(2,1)S(1)} async-done(((bf16[1,4,2,4096]{3,2,0,1:T(2,128)(2,1)}), bf16[1,4,2,4096]{3,2,0,1:T(2,128)(2,1)S(1)}, u32[]{:S(2)}, u32[]{:S(2)}) %all-to-all-start.4) | async-done | bytes 65568 | tf_op jit(solution)/shard_map/all_to_all | solution.py:93
  86.2 1.1 %fusion.9 = bf16[8,4096]{1,0:T(8,128)(2,1)} fusion(bf16[8,4096,1]{1,0,2:T(8,128)(2,1)S(1)} %reshape.110, f32[8,8]{1,0:T(8,128)S(1)} %get-tuple-element.5, s32[8,8]{1,0:T(8,128)S(1)} %multiply_add_fusion, pred[8,8]{1,0:T(8,128)(4,1)S(1)} %get-tuple-element.6), kind=kOutput, calls=%fused_computation.11 | convolution fusion | flops 4686848 | bytes 131648 | tf_op jit(solution)/shard_map/tkm,md->tkd/dot_general | solution.py:102
  (31 shorter events, 0.8 us)
Async XLA Ops:
  6.5 59.6 %copy-start = (bf16[1,1024,1024]{2,1,0:T(8,128)(2,1)S(1)}, bf16[1,1024,1024]{2,1,0:T(8,128)(2,1)}, u32[]{:S(2)}) copy-start(bf16[1,1024,1024]{2,1,0:T(8,128)(2,1)} %param.17) | copy-start | bytes 6291460
  6.5 49.9 %all-gather.4.cloned.1.call-start = ((), (), s32[]{:S(2)}) async-start(), calls=%async_computation.5 | async-start | bytes 3932160 | tf_op jit(solution)/shard_map/all_gather | solution.py:60
  9.8 15.6 %all-to-all-start.1 = ((s32[4,1,2]{2,1,0:T(1,128)}), s32[4,1,2]{2,1,0:T(1,128)S(1)}, u32[]{:S(2)}, u32[]{:S(2)}) async-start(s32[4,1,2]{2,1,0:T(1,128)} %copy.39), calls=%async_computation.1 | async-start | bytes 4096 | tf_op jit(solution)/shard_map/all_to_all | solution.py:42
  17.8 7.6 %copy-start.2 = (s32[8,8]{1,0:T(8,128)S(1)}, s32[8,8]{1,0:T(8,128)}, u32[]{:S(2)}) copy-start(s32[8,8]{1,0:T(8,128)} %param.11) | copy-start | bytes 772
  17.8 7.6 %copy-start.3 = (s32[8,8]{1,0:T(8,128)S(1)}, s32[8,8]{1,0:T(8,128)}, u32[]{:S(2)}) copy-start(s32[8,8]{1,0:T(8,128)} %param.12) | copy-start | bytes 772
  25.4 11.7 %all-to-all-start = ((bf16[4,2,4096]{2,1,0:T(2,128)(2,1)}), bf16[4,2,4096]{2,1,0:T(2,128)(2,1)S(1)}, u32[]{:S(2)}, u32[]{:S(2)}) async-start(bf16[4,2,4096]{2,1,0:T(2,128)(2,1)} %copy.38), calls=%async_computation | async-start | bytes 131072 | tf_op jit(solution)/shard_map/all_to_all | solution.py:41
  37.1 13.8 %all-to-all-start.2 = ((bf16[4,2,12288]{2,1,0:T(2,128)(2,1)}), bf16[4,2,12288]{2,1,0:T(2,128)(2,1)S(1)}, u32[]{:S(2)}, u32[]{:S(2)}) async-start(bf16[4,2,12288]{2,1,0:T(2,128)(2,1)} %reshape.122), calls=%async_computation.2 | async-start | bytes 393216 | tf_op jit(solution)/shard_map/all_to_all | solution.py:70
  48.2 2.2 %copy-start.1 = (bf16[1,4096,256]{2,1,0:T(8,128)(2,1)S(1)}, bf16[1,4096,256]{2,1,0:T(8,128)(2,1)}, u32[]{:S(2)}) copy-start(bf16[1,4096,256]{2,1,0:T(8,128)(2,1)} %param.15) | copy-start | bytes 6291460
  67.3 7.4 %all-to-all-start.3 = ((bf16[4,4,2,1024]{3,2,1,0:T(2,128)(2,1)}), bf16[4,4,2,1024]{3,2,1,0:T(2,128)(2,1)S(1)}, u32[]{:S(2)}, u32[]{:S(2)}) async-start(bf16[4,4,2,1024]{3,2,1,0:T(2,128)(2,1)} %reshape.102), calls=%async_computation.3 | async-start | bytes 131072 | tf_op jit(solution)/shard_map/all_to_all | solution.py:92
  75.4 10.8 %all-to-all-start.4 = ((bf16[1,4,2,4096]{3,2,0,1:T(2,128)(2,1)}), bf16[1,4,2,4096]{3,2,0,1:T(2,128)(2,1)S(1)}, u32[]{:S(2)}, u32[]{:S(2)}) async-start(bf16[1,4,2,4096]{3,2,0,1:T(2,128)(2,1)} %bitcast.16), calls=%async_computation.4 | async-start | bytes 131072 | tf_op jit(solution)/shard_map/all_to_all | solution.py:93
Sparse Core Ops, SparseCore 0:
  8.9 31.2 all-gather.3
where the time goes:
time: 95 us; the launch traced here: 94.2 us
  starting transfers between devices  23.2 us (24%)
  blocking collectives  18.1 us (19%)
  local copies, waits for them, and re-layouts  16.5 us (17%)
  between operations  13.5 us (14%)
  waiting for transfers between devices  10.5 us (11%)
  matrix products  9.7 us (10%)
  other arithmetic  2.62 us (3%)
    unnamed x11, local copies, waits for them, and re-layouts  9.81 us
    all_gather x1, blocking collectives, per_device(): lax.all_gather(got_rows[None], 'dp', axis=0, tiled=True)  7.51 us
    all_to_all x1, starting transfers between devices, per_device(): lax.all_to_all(send_ten, 'expert', split_axis=0, concat_axis=0, tiled=True)  6.35 us
    all_to_all x1, waiting for transfers between devices, per_device(): lax.all_to_all(home_rows, 'expert', split_axis=1, concat_axis=0, tiled=True)  5.74 us
    all_gather x1, blocking collectives, per_device(): lax.all_gather(got_ten[None], 'dp', axis=0, tiled=True)  5.35 us
    all_gather x1, blocking collectives, per_device(): lax.all_gather(hidden, 'dp', axis=1, tiled=True)  5.24 us
    all_to_all x1, starting transfers between devices, per_device(): lax.all_to_all(home_rows, 'expert', split_axis=1, concat_axis=0, tiled=True)  5.1 us
    all_to_all x1, starting transfers between devices, per_device(): lax.all_to_all(send_rows, 'expert', split_axis=0, concat_axis=0, tiled=True)  5.1 us
  transfers between devices with their start and end apart: 6, of which 2 were waited for; matrix products, arithmetic and copies ran while one was open for 23% of the time, Pallas kernels for 0%

commit v1 on v0

--- a/solution.py
+++ b/solution.py
@@ -67,8 +67,11 @@
         page_pick[:, :, None] * products.reshape(slot_count, page_count, rank_extent), axis=1
     )
     shrink_low = shrink_result.astype(jnp.bfloat16)
-    expand_every_page = lax.all_to_all(
-        adapter_expand, "dp", split_axis=3, concat_axis=1, tiled=True
+    expand_every_page = jnp.concatenate(
+        lax.all_to_all(
+            jnp.stack(jnp.split(adapter_expand, lax.axis_size("dp"), axis=3)), "dp", 0, 0
+        ),
+        axis=1,
     )[0]
     hidden_part = expand_every_page.shape[2]
     expand_matrix = expand_every_page.reshape(tenants * rank_extent, hidden_part)

time: 95 us -> 85.2 us (0.90)
  local copies, waits for them, and re-layouts: 16.5 us -> 5.25 us
  other arithmetic: 2.62 us -> 4.13 us
    unnamed x11 -> x6, local copies, waits for them, and re-layouts: 9.81 us -> 0.02 us
    all_to_all x2 -> x0, local copies, waits for them, and re-layouts: 2.5 us -> none  [per_device(): lax.all_to_all(adapter_expand, 'dp', split_axis=3, concat_axis=1, tiled=T...]
  transfers between devices with their start and end apart: 6 -> 6, of which waited for: 2 -> 3; matrix products, arithmetic and copies ran while one was open for 23% -> 19% of each run, Pallas kernels for 0% -> 0%
where the time goes in v1:
time: 85.2 us; the launch traced here: 84.4 us
  starting transfers between devices  22.5 us (26%)
  blocking collectives  18.1 us (21%)
  between operations  13.5 us (16%)
  waiting for transfers between devices  11.2 us (13%)
  matrix products  9.7 us (11%)
  local copies, waits for them, and re-layouts  5.25 us (6%)
  other arithmetic  4.13 us (5%)
    all_gather x1, blocking collectives, per_device(): lax.all_gather(got_rows[None], 'dp', axis=0, tiled=True)  7.51 us
    all_to_all x1, starting transfers between devices, per_device(): lax.all_to_all(send_ten, 'expert', split_axis=0, concat_axis=0, tiled=True)  6.35 us
    all_to_all x1, waiting for transfers between devices, per_device(): lax.all_to_all(home_rows, 'expert', split_axis=1, concat_axis=0, tiled=True)  5.74 us
    all_gather x1, blocking collectives, per_device(): lax.all_gather(got_ten[None], 'dp', axis=0, tiled=True)  5.35 us
    all_gather x1, blocking collectives, per_device(): lax.all_gather(hidden, 'dp', axis=1, tiled=True)  5.24 us
    all_to_all x1, starting transfers between devices, per_device(): lax.all_to_all(home_rows, 'expert', split_axis=1, concat_axis=0, tiled=True)  5.11 us
    all_to_all x1, starting transfers between devices, per_device(): lax.all_to_all(send_rows, 'expert', split_axis=0, concat_axis=0, tiled=True)  4.39 us
    dot_general x1, matrix products, per_device(): lax.dot_general(slot_input, flat_pages, (((1,), (1,)), ((), ())), preferr...  4.25 us
  transfers between devices with their start and end apart: 6, of which 3 were waited for; matrix products, arithmetic and copies ran while one was open for 19% of the time, Pallas kernels for 0%

profile of v1, /device:TPU:0, one launch (start us, length us, event | category | flops | bytes accessed | tf_op | source)
XLA Modules:
  0.0 84.4 jit_solution(15228823958038971786)
XLA Ops:
  6.5 0.7 all-gather.4.cloned.1.call-update
  7.3 0.8 convert_reduce_fusion
  8.1 0.2 reduce_window_sum.11
  8.3 0.7 broadcast_add_fusion
  9.1 0.7 copy.29
  9.8 6.3 %all-to-all-start.1 = ((s32[4,1,2]{2,1,0:T(1,128)}), s32[4,1,2]{2,1,0:T(1,128)S(1)}, u32[]{:S(2)}, u32[]{:S(2)}) async-start(s32[4,1,2]{2,1,0:T(1,128)} %copy.29), calls=%async_computation.1 | async-start | bytes 4096 | tf_op jit(solution)/shard_map/all_to_all | solution.py:42
  16.1 1.0 %convolution_convert_fusion = bf16[4,2,4096]{2,0,1:T(4,128)(2,1)S(1)} fusion(bf16[8,4096]{1,0:T(8,128)(2,1)} %param.10, s32[4,8]{1,0:T(4,128)S(1)} %bitcast.59, pred[4,8]{1,0:T(4,128)(4,1)S(1)} %compare_bitcast_fusion), kind=kOutput, calls=%fused_computation.1 | convolution fusion | flops 557184 | bytes 131232 | tf_op jit(solution)/shard_map/ect,td->ecd/dot_general | solution.py:36
  17.1 0.7 copy.28
  17.8 0.7 dynamic-slice_bitcast_fusion
  18.5 0.9 %slice_bitcast_fusion.3 = (bf16[1,1,6,16,256]{4,3,2,1,0:T(8,128)(2,1)S(1)}, bf16[1,1,6,16,256]{4,3,2,1,0:T(8,128)(2,1)S(1)}, bf16[1,1,6,16,256]{4,3,2,1,0:T(8,128)(2,1)S(1)}, bf16[1,1,6,16,256]{4,3,2,1,0:T(8,128)(2,1)S(1)}) fusion(bf16[1,6,16,1024]{3,2,1,0:T(8,128)(2,1)} %param.19), kind=kLoop, calls=%fused_computation.24 | loop fusion | bytes 393216 | tf_op jit(solution)/shard_map/stack | solution.py:72
  19.4 0.7 pad_maximum_fusion
  20.1 0.7 multiply_select_fusion
  20.9 0.7 all-to-all-done.1
  21.5 4.4 %all-to-all-start = ((bf16[4,2,4096]{2,1,0:T(2,128)(2,1)}), bf16[4,2,4096]{2,1,0:T(2,128)(2,1)S(1)}, u32[]{:S(2)}, u32[]{:S(2)}) async-start(bf16[4,2,4096]{2,1,0:T(2,128)(2,1)} %copy.28), calls=%async_computation | async-start | bytes 131072 | tf_op jit(solution)/shard_map/all_to_all | solution.py:41
  25.9 5.3 %all-gather.1 = s32[16,1,2]{2,1,0:T(1,128)S(1)} all-gather(s32[4,1,2]{2,1,0:T(1,128)S(1)} %all-to-all-done.1), channel_id=3, replica_groups=mesh['group'=2,'expert'=4,'dp'=4] {'dp'}, dimensions={0}, use_global_device_ids=true | all-gather | bytes 160 | tf_op jit(solution)/shard_map/all_gather | solution.py:46
  31.3 0.6 broadcast.74
  31.9 0.7 reduce.3
  32.7 3.4 %all-to-all-start.2 = ((bf16[4,1,6,16,256]{4,3,2,1,0:T(8,128)(2,1)}), bf16[4,1,6,16,256]{4,3,2,1,0:T(8,128)(2,1)S(1)}, u32[]{:S(2)}, u32[]{:S(2)}) async-start(bf16[4,1,6,16,256]{4,3,2,1,0:T(8,128)(2,1)} %pad_maximum_fusion), calls=%async_computation.2 | async-start | bytes 393216 | tf_op jit(solution)/shard_map/all_to_all | solution.py:71
  36.1 7.5 %all-gather = bf16[16,2,4096]{2,1,0:T(2,128)(2,1)S(1)} all-gather(bf16[4,2,4096]{2,1,0:T(2,128)(2,1)S(1)} %all-to-all-done), channel_id=2, replica_groups=mesh['group'=2,'expert'=4,'dp'=4] {'dp'}, dimensions={0}, use_global_device_ids=true | all-gather | bytes 327680 | tf_op jit(solution)/shard_map/all_gather | solution.py:45
  43.9 2.2 %fusion.5 = f32[32,256]{1,0:T(8,128)S(1)} fusion(bf16[32,4096]{1,0:T(8,128)(2,1)S(1)} %reshape.100, bf16[1,4096,256]{2,1,0:T(8,128)(2,1)} %param.16), kind=kOutput, calls=%fused_computation.7 | convolution fusion | flops 67108864 | bytes 2392064 | tf_op jit(solution)/shard_map/dot_general | solution.py:85
  46.1 0.5 fusion.7
  46.6 4.2 %fusion.16 = bf16[32,16]{0,1:T(8,128)(2,1)S(1)} fusion(bf16[32,4096,1]{1,0,2:T(8,128)(2,1)S(1)} %reshape.108, bf16[1,24,16,4096]{3,2,0,1:T(8,128)(2,1)} %all-gather.4.cloned.1.call-done, f32[32,24]{0,1:T(8,128)S(1)} %fusion.27), kind=kOutput, calls=%fused_computation.14 | convolution fusion | flops 100687360 | bytes 3411968 | tf_op jit(solution)/shard_map/dot_general | solution.py:63
  50.9 0.2 fusion.20
  51.1 5.2 %all_gather.15 = bf16[32,1024]{1,0:T(8,128)(2,1)S(1)} all-gather(bf16[32,256]{1,0:T(8,128)(2,1)S(1)} %fusion.20), channel_id=1, replica_groups=mesh['group'=2,'expert'=4,'dp'=4] {'dp'}, dimensions={1}, use_global_device_ids=true | all-gather | bytes 81920 | tf_op jit(solution)/shard_map/all_gather | solution.py:90
  56.3 0.5 fusion.13
  56.8 0.7 reshape.101
  57.5 3.3 %all-to-all-start.3 = ((bf16[4,4,2,1024]{3,2,1,0:T(2,128)(2,1)}), bf16[4,4,2,1024]{3,2,1,0:T(2,128)(2,1)S(1)}, u32[]{:S(2)}, u32[]{:S(2)}) async-start(bf16[4,4,2,1024]{3,2,1,0:T(2,128)(2,1)} %reshape.101), calls=%async_computation.3 | async-start | bytes 131072 | tf_op jit(solution)/shard_map/all_to_all | solution.py:95
  60.9 4.0 %all-to-all-done.3 = bf16[4,4,2,1024]{3,2,1,0:T(2,128)(2,1)S(1)} async-done(((bf16[4,4,2,1024]{3,2,1,0:T(2,128)(2,1)}), bf16[4,4,2,1024]{3,2,1,0:T(2,128)(2,1)S(1)}, u32[]{:S(2)}, u32[]{:S(2)}) %all-to-all-start.3) | async-done | bytes 65568 | tf_op jit(solution)/shard_map/all_to_all | solution.py:95
  64.9 0.7 copy.35
  65.5 5.1 %all-to-all-start.4 = ((bf16[1,4,2,4096]{3,2,0,1:T(2,128)(2,1)}), bf16[1,4,2,4096]{3,2,0,1:T(2,128)(2,1)S(1)}, u32[]{:S(2)}, u32[]{:S(2)}) async-start(bf16[1,4,2,4096]{3,2,0,1:T(2,128)(2,1)} %bitcast.18), calls=%async_computation.4 | async-start | bytes 131072 | tf_op jit(solution)/shard_map/all_to_all | solution.py:96
  70.7 5.7 %all-to-all-done.4 = bf16[1,4,2,4096]{3,2,0,1:T(2,128)(2,1)S(1)} async-done(((bf16[1,4,2,4096]{3,2,0,1:T(2,128)(2,1)}), bf16[1,4,2,4096]{3,2,0,1:T(2,128)(2,1)S(1)}, u32[]{:S(2)}, u32[]{:S(2)}) %all-to-all-start.4) | async-done | bytes 65568 | tf_op jit(solution)/shard_map/all_to_all | solution.py:96
  76.4 1.1 %fusion.9 = bf16[8,4096]{1,0:T(8,128)(2,1)} fusion(bf16[8,4096,1]{1,0,2:T(8,128)(2,1)S(1)} %reshape.109, f32[8,8]{1,0:T(8,128)S(1)} %get-tuple-element.5, s32[8,8]{1,0:T(8,128)S(1)} %multiply_add_fusion, pred[8,8]{1,0:T(8,128)(4,1)S(1)} %get-tuple-element.6), kind=kOutput, calls=%fused_computation.11 | convolution fusion | flops 4686848 | bytes 131648 | tf_op jit(solution)/shard_map/tkm,md->tkd/dot_general | solution.py:105
  (26 shorter events, 0.8 us)
Async XLA Ops:
  6.5 49.8 %copy-start = (bf16[1,1024,1024]{2,1,0:T(8,128)(2,1)S(1)}, bf16[1,1024,1024]{2,1,0:T(8,128)(2,1)}, u32[]{:S(2)}) copy-start(bf16[1,1024,1024]{2,1,0:T(8,128)(2,1)} %param.17) | copy-start | bytes 6291460
  6.5 40.0 %all-gather.4.cloned.1.call-start = ((), (), s32[]{:S(2)}) async-start(), calls=%async_computation.5 | async-start | bytes 3932160 | tf_op jit(solution)/shard_map/all_gather | solution.py:60
  9.8 11.8 %all-to-all-start.1 = ((s32[4,1,2]{2,1,0:T(1,128)}), s32[4,1,2]{2,1,0:T(1,128)S(1)}, u32[]{:S(2)}, u32[]{:S(2)}) async-start(s32[4,1,2]{2,1,0:T(1,128)} %copy.29), calls=%async_computation.1 | async-start | bytes 4096 | tf_op jit(solution)/shard_map/all_to_all | solution.py:42
  21.5 11.2 %all-to-all-start = ((bf16[4,2,4096]{2,1,0:T(2,128)(2,1)}), bf16[4,2,4096]{2,1,0:T(2,128)(2,1)S(1)}, u32[]{:S(2)}, u32[]{:S(2)}) async-start(bf16[4,2,4096]{2,1,0:T(2,128)(2,1)} %copy.28), calls=%async_computation | async-start | bytes 131072 | tf_op jit(solution)/shard_map/all_to_all | solution.py:41
  32.7 18.2 %all-to-all-start.2 = ((bf16[4,1,6,16,256]{4,3,2,1,0:T(8,128)(2,1)}), bf16[4,1,6,16,256]{4,3,2,1,0:T(8,128)(2,1)S(1)}, u32[]{:S(2)}, u32[]{:S(2)}) async-start(bf16[4,1,6,16,256]{4,3,2,1,0:T(8,128)(2,1)} %pad_maximum_fusion), calls=%async_computation.2 | async-start | bytes 393216 | tf_op jit(solution)/shard_map/all_to_all | solution.py:71
  43.8 2.2 %copy-start.1 = (bf16[1,4096,256]{2,1,0:T(8,128)(2,1)S(1)}, bf16[1,4096,256]{2,1,0:T(8,128)(2,1)}, u32[]{:S(2)}) copy-start(bf16[1,4096,256]{2,1,0:T(8,128)(2,1)} %param.15) | copy-start | bytes 6291460
  50.8 10.0 %copy-start.2 = (s32[8,8]{1,0:T(8,128)S(1)}, s32[8,8]{1,0:T(8,128)}, u32[]{:S(2)}) copy-start(s32[8,8]{1,0:T(8,128)} %param.11) | copy-start | bytes 772
  57.5 7.4 %all-to-all-start.3 = ((bf16[4,4,2,1024]{3,2,1,0:T(2,128)(2,1)}), bf16[4,4,2,1024]{3,2,1,0:T(2,128)(2,1)S(1)}, u32[]{:S(2)}, u32[]{:S(2)}) async-start(bf16[4,4,2,1024]{3,2,1,0:T(2,128)(2,1)} %reshape.101), calls=%async_computation.3 | async-start | bytes 131072 | tf_op jit(solution)/shard_map/all_to_all | solution.py:95
  65.5 10.9 %all-to-all-start.4 = ((bf16[1,4,2,4096]{3,2,0,1:T(2,128)(2,1)}), bf16[1,4,2,4096]{3,2,0,1:T(2,128)(2,1)S(1)}, u32[]{:S(2)}, u32[]{:S(2)}) async-start(bf16[1,4,2,4096]{3,2,0,1:T(2,128)(2,1)} %bitcast.18), calls=%async_computation.4 | async-start | bytes 131072 | tf_op jit(solution)/shard_map/all_to_all | solution.py:96
Sparse Core Ops, SparseCore 0:
  8.9 31.2 all-gather.3
